TPU v7x, 256 devices: a whole 4x4x8 slice. The times are simulated.
256 devices in a mesh: dp: 4 (over x), seq: 64 (over z, y, core).
Axes of the slice: x: 4, y: 4, z: 8, core: 2. Of those that a mesh axis runs over, the one named last changes fastest.
Arguments:
- streams: bfloat16 [3, 4, 8192, 4096], P(None, 'dp', 'seq'), may hold values from -6 to 6
- short_filter: float32 [3, 3, 4096], P(None, None, 'dp'), may hold values from -3.5 to 3.5
- decay_rate: float32 [2, 4096], P(None, 'dp'), may hold values from 1.2207031e-06 to 0.05
- pole_angle: float32 [2, 4096], P(None, 'dp'), may hold values from -3.140625 to 3.140625
- residue_re: float32 [2, 4096], P(None, 'dp'), may hold values from -6 to 6
- residue_im: float32 [2, 4096], P(None, 'dp'), may hold values from -6 to 6
- skip_gain: float32 [4096], P('dp'), may hold values from -6 to 6
- doc_starts: int32 [4, 8], P('dp'), may hold values from 0 to 8191, as said below
Outputs:
- mixed: bfloat16 [4, 8192, 4096], P('dp', 'seq')
Inputs may be any that keep to these rules, and one draw needn't show every extreme that they name: `doc_starts`: each row starts with 0 and rises strictly; the last document of every sequence is one position long.
All inputs are finite; a program needn't handle non-finite values.
Results may differ from a plain program's by a relative error of at most 0.0045.
Values may be sent and summed in bfloat16 or wider, within the bound.
A program may use at most 128 MiB of HBM per device.

v0:
```python
import jax
import jax.numpy as jnp
from jax import lax
from jax.sharding import PartitionSpec as P

block_len = 32


def from_behind(x, axis, by):
    count = lax.axis_size(axis)
    pairs = [(i, i + by) for i in range(count) if 0 <= i + by < count]
    return lax.ppermute(x, axis, pairs)


def prefix_2(part, axis, combine, identity):
    place = lax.axis_index(axis)
    gathered = jax.tree.map(lambda a: lax.all_gather(a, axis), part)
    state = jax.tree.map(lambda a, e: jnp.zeros_like(a) + jnp.asarray(e, a.dtype), part, identity)

    def one(turn, state):
        return combine(
            state, jax.tree.map(lambda a: lax.dynamic_index_in_dim(a, turn, 0, False), gathered)
        )

    return lax.fori_loop(0, place, one, state)


def pole_power(decay, rotation, powers):
    magnitude = jnp.exp(-decay * powers)
    return (magnitude * jnp.cos(rotation * powers), magnitude * jnp.sin(rotation * powers))


def segment_of(positions, starts):
    return jnp.sum((positions[..., None] >= starts).astype(jnp.int32), axis=-1) - 1


def local(
    streams, short_filter, decay_rate, pole_angle, residue_re, residue_im, skip_gain, doc_starts
):
    short_filter, decay_rate, pole_angle, residue_re, residue_im, skip_gain = (
        lax.all_gather(short_filter, "dp", axis=2, tiled=True),
        lax.all_gather(decay_rate, "dp", axis=1, tiled=True),
        lax.all_gather(pole_angle, "dp", axis=1, tiled=True),
        lax.all_gather(residue_re, "dp", axis=1, tiled=True),
        lax.all_gather(residue_im, "dp", axis=1, tiled=True),
        lax.all_gather(skip_gain, "dp", axis=0, tiled=True),
    )
    tok_rows = streams.shape[2]
    channels = streams.shape[3]
    modes = decay_rate.shape[0]
    my_index = lax.axis_index("seq")
    offset = my_index * tok_rows
    starts = doc_starts[0]
    rim_rows = streams[:, :, tok_rows - 2 :, :]
    before = from_behind(rim_rows, "seq", 1)
    extended = jnp.concatenate([before, streams], axis=2)[:, 0]
    filtered = (
        short_filter[0][:, None, :] * extended[:, 2:]
        + short_filter[1][:, None, :] * extended[:, 1:-1]
        + short_filter[2][:, None, :] * extended[:, :-2]
    )
    product = filtered[0] * filtered[1]
    out_gate = filtered[2]
    positions = offset + jnp.arange(tok_rows, dtype=jnp.int32)
    seg_ids = segment_of(positions, starts)
    seg_before = segment_of(offset - 1 + jnp.zeros((1,), jnp.int32), starts)[0]
    nblocks = tok_rows // block_len
    local_steps = jnp.arange(block_len, dtype=jnp.float32)[:, None, None]
    fwd_re, fwd_im = pole_power(decay_rate, pole_angle, local_steps)
    back_re, back_im = pole_power(-decay_rate, -pole_angle, local_steps)
    blocked = product.reshape(nblocks, block_len, 1, channels)
    lifted = jnp.concatenate([blocked * back_re, blocked * back_im], axis=2)
    lifted = lifted.reshape(nblocks, block_len, 2 * modes * channels)
    seg_blocks = seg_ids.reshape(nblocks, block_len)
    causal = jnp.arange(block_len)[:, None] >= jnp.arange(block_len)[None, :]
    within = (causal[None] & (seg_blocks[:, :, None] == seg_blocks[:, None, :])).astype(jnp.float32)
    summed = jnp.einsum("bts,bsk->btk", within, lifted, precision=lax.Precision.HIGHEST)
    summed = summed.reshape(nblocks, block_len, 2 * modes, channels)
    sum_re = summed[:, :, :modes]
    sum_im = summed[:, :, modes:]
    state_re = fwd_re * sum_re - fwd_im * sum_im
    state_im = fwd_re * sum_im + fwd_im * sum_re
    step_re, step_im = pole_power(decay_rate, pole_angle, jnp.float32(block_len))
    entry_seg = jnp.concatenate([seg_before[None], seg_blocks[:-1, -1]])
    keeps_last = (seg_blocks[:, -1] == entry_seg).astype(jnp.float32)

    def advance(running, inputs):
        run_re, run_im = running
        last_re, last_im, kept_now = inputs
        next_re = last_re + kept_now * (step_re * run_re - step_im * run_im)
        next_im = last_im + kept_now * (step_re * run_im + step_im * run_re)
        return ((next_re, next_im), (run_re, run_im))

    zero_state = jnp.zeros((modes, channels), jnp.float32)
    (end_re, end_im), (entry_re, entry_im) = lax.scan(
        advance, (zero_state, zero_state), (state_re[:, -1], state_im[:, -1], keeps_last)
    )
    lead_re, lead_im = pole_power(decay_rate, pole_angle, local_steps + 1.0)
    joined = (seg_blocks == entry_seg[:, None]).astype(jnp.float32)[:, :, None, None]
    state_re = state_re + joined * (lead_re * entry_re[:, None] - lead_im * entry_im[:, None])
    state_im = state_im + joined * (lead_re * entry_im[:, None] + lead_im * entry_re[:, None])
    whole_re, whole_im = pole_power(decay_rate, pole_angle, jnp.float32(tok_rows))
    keep_all = (seg_ids[-1] == seg_before).astype(jnp.float32)

    def combine(earlier, latter):
        early_are, early_aim, early_sre, early_sim = earlier
        late_are, late_aim, late_sre, late_sim = latter
        return (
            late_are * early_are - late_aim * early_aim,
            late_are * early_aim + late_aim * early_are,
            late_sre + late_are * early_sre - late_aim * early_sim,
            late_sim + late_are * early_sim + late_aim * early_sre,
        )

    unit_state = jnp.ones_like(end_re)
    prefix = prefix_2(
        (keep_all * whole_re, keep_all * whole_im, end_re, end_im),
        "seq",
        combine,
        (unit_state, zero_state, zero_state, zero_state),
    )
    inflow_re = prefix[2]
    inflow_im = prefix[3]
    all_steps = (
        jnp.arange(tok_rows, dtype=jnp.float32).reshape(nblocks, block_len)[:, :, None, None] + 1.0
    )
    enter_re, enter_im = pole_power(decay_rate, pole_angle, all_steps)
    reach = (seg_blocks == seg_before).astype(jnp.float32)[:, :, None, None]
    state_re = state_re + reach * (enter_re * inflow_re - enter_im * inflow_im)
    state_im = state_im + reach * (enter_re * inflow_im + enter_im * inflow_re)
    norm_factor = jnp.sqrt(-jnp.expm1(-2.0 * decay_rate))
    long_part = jnp.sum(norm_factor * (residue_re * state_re - residue_im * state_im), axis=2)
    long_part = long_part.reshape(tok_rows, channels)
    response = skip_gain * product + long_part
    return (out_gate * response).astype(jnp.bfloat16)[None]


def solution(mesh):
    placed = (
        P(None, "dp", "seq", None),
        P(None, None, "dp"),
        P(None, "dp"),
        P(None, "dp"),
        P(None, "dp"),
        P(None, "dp"),
        P("dp"),
        P("dp", None),
    )
    return jax.shard_map(
        local, mesh=mesh, in_specs=placed, out_specs=P("dp", "seq", None), check_vma=False
    )
```

profile of v0, /device:TPU:249, one launch (start us, length us, event | category | flops | bytes accessed | tf_op | source)
XLA Modules:
  0.0 430.3 jit_solution(6064338715635104115)
XLA Ops:
  6.5 1.3 fusion.14
  10.5 9.6 %all_gather.46 = f32[2,4096]{1,0:T(2,128)S(1)} all-gather(f32[2,1024]{1,0:T(2,128)} %param.15), channel_id=1, replica_groups=mesh['dp'=4,'seq'=64] {'dp'}, dimensions={1}, use_global_device_ids=true | all-gather | bytes 40960 | tf_op jit(solution)/shard_map/all_gather | solution.py:43
  20.1 9.2 %all_gather.44 = f32[2,4096]{1,0:T(2,128)S(1)} all-gather(f32[2,1024]{1,0:T(2,128)} %param.14), channel_id=1, replica_groups=mesh['dp'=4,'seq'=64] {'dp'}, dimensions={1}, use_global_device_ids=true | all-gather | bytes 40960 | tf_op jit(solution)/shard_map/all_gather | solution.py:42
  29.3 1.7 multiply_bitcast_fusion
  31.0 1.0 slice.69
  32.0 1.3 collective-permute-start
  33.8 16.3 %cosine_multiply_fusion = (f32[32,2,4096]{2,1,0:T(2,128)}, f32[32,2,4096]{2,1,0:T(2,128)}) fusion(f32[2,4096]{1,0:T(2,128)S(1)} %get-tuple-element.233, f32[2,4096]{1,0:T(2,128)S(1)} %all_gather.44), kind=kLoop, calls=%fused_computation.37 | loop fusion | flops 1048576 | bytes 2162688 | tf_op jit(solution)/shard_map/mul | solution.py:30
  50.2 9.8 %all_gather.42 = f32[3,3,4096]{2,1,0:T(4,128)S(1)} all-gather(f32[3,3,1024]{2,1,0:T(4,128)} %param.13), channel_id=1, replica_groups=mesh['dp'=4,'seq'=64] {'dp'}, dimensions={2}, use_global_device_ids=true | all-gather | bytes 184320 | tf_op jit(solution)/shard_map/all_gather | solution.py:41
  60.0 8.6 %fusion.6 = (f32[32,2,4096]{2,0,1:T(8,128)S(1)}, f32[32,2,4096]{2,0,1:T(8,128)S(1)}, f32[32,2,4096]{2,0,1:T(8,128)}, f32[32,2,4096]{2,0,1:T(8,128)}) fusion(f32[32]{0:T(128)S(1)} %iota_add_fusion, f32[2,4096]{1,0:T(2,128)S(1)} %all_gather.46, f32[2,4096]{1,0:T(2,128)S(1)} %get-tuple-element.234), kind=kLoop, calls=%fused_computation.32 | loop fusion | flops 2097152 | bytes 4259968 | tf_op jit(solution)/shard_map/mul | solution.py:30
  68.7 2.7 maximum_bitcast_fusion
  71.4 2.1 multiply_add_fusion
  73.8 1.7 copy-done.4
  75.6 1.1 copy-done.5
  76.7 3.9 broadcast_multiply_fusion.1
  80.5 9.7 %pad_maximum_fusion = f32[4,32,4,4096]{3,2,1,0:T(4,128)} fusion(f32[4,32,2,4096]{3,2,1,0:T(2,128)} %get-tuple-element.218, f32[4,32,2,4096]{3,2,1,0:T(2,128)S(1)} %get-tuple-element.217), kind=kLoop, calls=%fused_computation.14 | loop fusion | flops 2097152 | bytes 16777216 | tf_op jit(solution)/shard_map/concatenate | solution.py:72
  90.3 11.0 %reshape.158 = f32[4,32,16384]{2,1,0:T(8,128)} reshape(f32[4,32,4,4096]{3,2,1,0:T(4,128)} %pad_maximum_fusion) | data formatting | bytes 16777216 | tf_op jit(solution)/shard_map/reshape | solution.py:73
  101.3 10.8 %fusion.8 = f32[4,32,16384]{2,1,0:T(8,128)} fusion(f32[4,32,16384]{2,1,0:T(8,128)} %reshape.158, s32[4,32]{1,0:T(4,128)S(1)} %sub.35, pred[32,32]{1,0:T(8,128)(4,1)S(1)} %iota_compare_fusion), kind=kOutput, calls=%fused_computation.48 | convolution fusion | flops 805314560 | bytes 16778752 | tf_op jit(solution)/shard_map/bts,bsk->btk/dot_general | solution.py:77
  112.1 10.8 %reshape.159 = f32[4,32,4,4096]{3,2,1,0:T(4,128)} reshape(f32[4,32,16384]{2,1,0:T(8,128)} %fusion.8) | data formatting | bytes 16777216 | tf_op jit(solution)/shard_map/reshape | solution.py:78
  122.9 11.1 %fusion.15 = (f32[4,32,2,4096]{3,2,1,0:T(2,128)S(1)}, f32[4,32,2,4096]{3,2,1,0:T(2,128)}) fusion(f32[4,32,4,4096]{3,2,1,0:T(4,128)} %reshape.159), kind=kLoop, calls=%fused_computation.75 | loop fusion | bytes 16777216 | tf_op jit(solution)/shard_map/slice | solution.py:79
  134.0 7.8 %multiply_subtract_fusion = (f32[4,32,2,4096]{3,1,2,0:T(8,128)S(1)}, f32[4,32,2,4096]{3,1,2,0:T(8,128)S(1)}) fusion(f32[4,32,2,4096]{3,2,1,0:T(2,128)} %get-tuple-element.216, f32[4,32,2,4096]{3,2,1,0:T(2,128)S(1)} %get-tuple-element.215, f32[32,2,4096]{2,0,1:T(8,128)S(1)} %copy-done.3, f32[32,2,4096]{2,0,1:T(8,128)} %get-tuple-element.225), kind=kLoop, calls=%fused_computation.22 | loop fusion | flops 6291456 | bytes 18874368 | tf_op jit(solution)/shard_map/sub | solution.py:81
  141.9 2.0 copy-done.1
  144.0 1.1 copy-done.2
  145.5 7.9 %while.33 = (s32[]{:T(128)}, f32[2,4096]{1,0:T(2,128)S(1)}, f32[2,4096]{1,0:T(2,128)S(1)}, f32[4,2,4096]{2,1,0:T(2,128)S(1)}, f32[4,2,4096]{2,1,0:T(2,128)}, /*i...) while((s32[]{:T(128)}, f32[2,4096]{1,0:T(2,128)S(1)}, ...), condition=%wide.region_3.4_spmd.clone, body=%wide.region_2.3_spmd.clone.sunk | while | flops 114691 | bytes 393876 | solution.py:95
  154.6 9.0 %all_gather.43 = f32[4096]{0:T(1024)S(1)} all-gather(f32[1024]{0:T(1024)S(1)} %copy-done.10), channel_id=1, replica_groups=mesh['dp'=4,'seq'=64] {'dp'}, dimensions={0}, use_global_device_ids=true | all-gather | bytes 20480 | tf_op jit(solution)/shard_map/all_gather | solution.py:46
  163.7 9.6 %all_gather.45 = f32[2,4096]{1,0:T(2,128)S(1)} all-gather(f32[2,1024]{1,0:T(2,128)S(1)} %copy-done.8), channel_id=1, replica_groups=mesh['dp'=4,'seq'=64] {'dp'}, dimensions={1}, use_global_device_ids=true | all-gather | bytes 40960 | tf_op jit(solution)/shard_map/all_gather | solution.py:44
  173.2 9.0 %all_gather.55 = f32[2,4096]{1,0:T(2,128)S(1)} all-gather(f32[2,1024]{1,0:T(2,128)S(1)} %copy-done.9), channel_id=1, replica_groups=mesh['dp'=4,'seq'=64] {'dp'}, dimensions={1}, use_global_device_ids=true | all-gather | bytes 40960 | tf_op jit(solution)/shard_map/all_gather | solution.py:45
  182.4 6.7 %all-gather.17.cloned.1.call-done = f32[64,2,4096]{2,1,0:T(2,128)} async-done(((f32[1,2,4096]{2,1,0:T(2,128)}), f32[64,2,4096]{2,1,0:T(2,128)}) %all-gather.17.cloned.1.call-update) | async-done | bytes 2097168 | tf_op jit(solution)/shard_map/all_gather | solution.py:17
  189.1 77.8 %all-gather.13.cloned.1.call-done = f32[64,2,4096]{2,1,0:T(2,128)} async-done(((f32[1,2,4096]{2,1,0:T(2,128)}), f32[64,2,4096]{2,1,0:T(2,128)}) %all-gather.13.cloned.1.call-update) | async-done | bytes 2097168 | tf_op jit(solution)/shard_map/all_gather | solution.py:17
  266.9 77.6 %all-gather.19.cloned.1.call-done = f32[64,2,4096]{2,1,0:T(2,128)} async-done(((f32[1,2,4096]{2,1,0:T(2,128)}), f32[64,2,4096]{2,1,0:T(2,128)}) %all-gather.19.cloned.1.call-update) | async-done | bytes 2097168 | tf_op jit(solution)/shard_map/all_gather | solution.py:17
  344.5 56.3 %while.32 = (s32[]{:T(128)}, f32[2,4096]{1,0:T(2,128)S(1)}, f32[2,4096]{1,0:T(2,128)S(1)}, s32[]{:T(128)}, f32[64,2,4096]{2,1,0:T(2,128)}, /*index=5*/f32[64,2,4...) while((s32[]{:T(128)}, f32[2,4096]{1,0:T(2,128)S(1)}, ...), condition=%wide.region_5.6_spmd, body=%wide.region_4.5_spmd.sunk | while | flops 65541 | bytes 262291 | solution.py:25
  344.5 0.9 fusion.18
  345.4 0.9 fusion.18
  347.2 0.9 fusion.18
  348.1 0.9 fusion.18
  349.0 0.9 fusion.18
  351.7 0.9 fusion.18
  352.6 0.9 fusion.18
  355.3 0.9 fusion.18
  358.8 0.9 fusion.18
  359.8 0.9 fusion.18
  362.4 0.9 fusion.18
  363.3 0.9 fusion.18
  366.0 0.9 fusion.18
  366.9 0.9 fusion.18
  369.6 0.9 fusion.18
  372.2 0.9 fusion.18
  400.8 21.4 %multiply_reduce_fusion = f32[4,32,4096]{2,1,0:T(8,128)S(1)} fusion(f32[4,32,2,4096]{3,1,2,0:T(8,128)} %copy-done.2, f32[4,32,2,4096]{3,1,2,0:T(8,128)} %copy-done.1, f32[2,4096]{1,0:T(2,128)S(1)} %all_gather.55, f32[2,4096]{1,0:T(2,128)S(1)} %get-tuple-element.135, f32[2,4096]{1,0:T(2,128)S(1)} %get-tuple-element.134, f32[2,4096]{1,0:T(2,128)S(1)} %all_gather.46, ...), kind=kLoop, calls=%fused_computation.20 | loop fusion | flops 29884416 | bytes 13075968 | tf_op jit(solution)/shard_map/reduce_sum | solution.py:132
  422.2 1.6 fusion.5
  (115 shorter events, 52.8 us)
Async XLA Ops:
  6.5 175.8 %all-gather.15.cloned.1.call-start = ((), (), s32[]{:S(2)}) async-start(), calls=%async_computation.1 | async-start | bytes 2129920 | tf_op jit(solution)/shard_map/all_gather | solution.py:17
  31.0 158.1 %all-gather.17.cloned.1.call-start = ((), (), s32[]{:S(2)}) async-start(), calls=%async_computation.2 | async-start | bytes 2129920 | tf_op jit(solution)/shard_map/all_gather | solution.py:17
  32.0 36.7 %collective-permute-start = (bf16[3,1,2,4096]{3,2,0,1:T(2,128)(2,1)S(1)}, bf16[3,1,2,4096]{3,2,0,1:T(2,128)(2,1)S(1)}, u32[]{:S(2)}, u32[]{:S(2)}) collective-permute-start(bf16[3,1,2,4096]{3,2,0,1:T(2,128)(2,1)S(1)} %slice.69), channel_id=1, source_target_pairs={{0,1},{1,2},{2,3},{3,4},{4,5},{5,6},{6,7},{7,8},{8,9},{9,10},{10,1... | collective-permute-start | bytes 147464 | tf_op jit(solution)/shard_map/ppermute | solution.py:12
  33.3 233.5 %all-gather.13.cloned.1.call-start = ((), (), s32[]{:S(2)}) async-start(), calls=%async_computation | async-start | bytes 2129920 | tf_op jit(solution)/shard_map/all_gather | solution.py:17
  73.5 7.0 %copy-start = (f32[3,128,4096]{2,1,0:T(8,128)}, f32[3,128,4096]{2,1,0:T(8,128)S(1)}, u32[]{:S(2)}) copy-start(f32[3,128,4096]{2,1,0:T(8,128)S(1)} %multiply_add_fusion) | copy-start | bytes 18874372
  73.6 2.0 copy-start.4
  73.6 3.1 copy-start.5
  122.9 11.1 %copy-start.3 = (f32[32,2,4096]{2,0,1:T(8,128)S(1)}, f32[32,2,4096]{2,0,1:T(8,128)}, u32[]{:S(2)}) copy-start(f32[32,2,4096]{2,0,1:T(8,128)} %get-tuple-element.224) | copy-start | bytes 3145732
  134.0 20.6 %copy-start.10 = (f32[1024]{0:T(1024)S(1)}, f32[1024]{0:T(1024)}, u32[]{:S(2)}) copy-start(f32[1024]{0:T(1024)} %param.18) | copy-start | bytes 12292
  134.0 29.7 %copy-start.8 = (f32[2,1024]{1,0:T(2,128)S(1)}, f32[2,1024]{1,0:T(2,128)}, u32[]{:S(2)}) copy-start(f32[2,1024]{1,0:T(2,128)} %param.16) | copy-start | bytes 24580
  134.0 39.2 %copy-start.9 = (f32[2,1024]{1,0:T(2,128)S(1)}, f32[2,1024]{1,0:T(2,128)}, u32[]{:S(2)}) copy-start(f32[2,1024]{1,0:T(2,128)} %param.17) | copy-start | bytes 24580
  141.8 2.0 copy-start.1
  141.8 3.3 copy-start.2
  153.4 0.6 copy-start.6
  153.4 0.7 copy-start.7
  154.0 190.4 %all-gather.19.cloned.1.call-start = ((), (), s32[]{:S(2)}) async-start(), calls=%async_computation.3 | async-start | bytes 2129920 | tf_op jit(solution)/shard_map/all_gather | solution.py:17
  400.8 21.4 %slice-start = ((s8[6291456]{0:T(1024)(128)(4,1)}), s8[4194304]{0:T(1024)(128)(4,1)S(1)}, s32[]{:S(2)}) async-start(s8[6291456]{0:T(1024)(128)(4,1)} %bitcast.73), calls=%async_computation.4 | async-start | bytes 8388608
  400.8 21.4 %slice-start.1 = ((s8[6291456]{0:T(1024)(128)(4,1)}), s8[2097152]{0:T(1024)(128)(4,1)S(1)}, s32[]{:S(2)}) async-start(s8[6291456]{0:T(1024)(128)(4,1)} %bitcast.73), calls=%async_computation.5 | async-start | bytes 4194304
Sparse Core Ops, SparseCore 0:
  31.1 80.2 all-gather.14
  114.1 74.9 all-gather.16
  191.9 74.9 all-gather.12
  269.5 74.9 all-gather.18
where the time goes:
time: 436 us; the launch traced here: 430 us
  waiting for transfers between devices  163 us (37%)
  other arithmetic  139 us (32%)
  blocking collectives  56.2 us (13%)
  local copies, waits for them, and re-layouts  44.3 us (10%)
  between operations  14.7 us (3%)
  matrix products  10.8 us (2%)
    all_gather x4, waiting for transfers between devices, prefix_2(): gathered = jax.tree.map(lambda a: lax.all_gather(a, axis), part)  162 us
    add x63, other arithmetic, combine(): late_sim + late_are * early_sim + late_aim * early_sre  54.8 us
    mul x2, other arithmetic, pole_power(): magnitude * jnp.cos(rotation * powers)  24.9 us
    reduce_sum x1, other arithmetic, local(): jnp.sum(norm_factor * (residue_re * state_re - residue_im * state_im), ax...  21.4 us
    slice x1, local copies, waits for them, and re-layouts, local(): sum_re = summed[:, :, :modes]  11.1 us
    reshape x1, local copies, waits for them, and re-layouts, local(): lifted = lifted.reshape(nblocks, block_len, 2 * modes * channels)  11 us
    dot_general x1, matrix products, local(): jnp.einsum('bts,bsk->btk', within, lifted, precision=lax.Precision.HIGHEST)  10.8 us
    reshape x1, local copies, waits for them, and re-layouts, local(): summed = summed.reshape(nblocks, block_len, 2 * modes, channels)  10.8 us
  transfers between devices with their start and end apart: 5, of which 3 were waited for; matrix products, arithmetic and copies ran while one was open for 24% of the time, Pallas kernels for 0%

commit v1 on v0

--- a/solution.py
+++ b/solution.py
@@ -4,6 +4,25 @@
 from jax.sharding import PartitionSpec as P
 
 block_len = 32
+
+
+def gather_around(x, axis, dim):
+    size, mine, rows = (lax.axis_size(axis), lax.axis_index(axis), x.shape[dim])
+    forward = [(i, (i + 1) % size) for i in range(size)]
+    left = [(i, (i - 1) % size) for i in range(size)]
+    out = jnp.zeros((*x.shape[:dim], size * rows, *x.shape[dim + 1 :]), x.dtype)
+    out = lax.dynamic_update_slice_in_dim(out, x, mine * rows, axis=dim)
+    from_left = from_right = x
+    half = size // 2
+    for lap in range(1, half + 1):
+        from_left = lax.ppermute(from_left, axis, forward)
+        out = lax.dynamic_update_slice_in_dim(out, from_left, (mine - lap) % size * rows, axis=dim)
+        if lap < size - half:
+            from_right = lax.ppermute(from_right, axis, left)
+            out = lax.dynamic_update_slice_in_dim(
+                out, from_right, (mine + lap) % size * rows, axis=dim
+            )
+    return out
 
 
 def from_behind(x, axis, by):
@@ -42,7 +61,7 @@
         lax.all_gather(decay_rate, "dp", axis=1, tiled=True),
         lax.all_gather(pole_angle, "dp", axis=1, tiled=True),
         lax.all_gather(residue_re, "dp", axis=1, tiled=True),
-        lax.all_gather(residue_im, "dp", axis=1, tiled=True),
+        gather_around(residue_im, "dp", 1),
         lax.all_gather(skip_gain, "dp", axis=0, tiled=True),
     )
     tok_rows = streams.shape[2]

time: 436 us -> 436 us (level)
  blocking collectives: 56.2 us -> 46.6 us
  waiting for transfers between devices: 163 us -> 169 us
    all_gather x1 -> x0, blocking collectives: 9.03 us -> none  [local(): lax.all_gather(residue_im, 'dp', axis=1, tiled=True)]
  transfers between devices with their start and end apart: 5 -> 8, of which waited for: 3 -> 4; matrix products, arithmetic and copies ran while one was open for 24% -> 24% of each run, Pallas kernels for 0% -> 0%
where the time goes in v1:
time: 436 us; the launch traced here: 430 us
  waiting for transfers between devices  169 us (39%)
  other arithmetic  138 us (32%)
  blocking collectives  46.6 us (11%)
  local copies, waits for them, and re-layouts  44.3 us (10%)
  between operations  14.7 us (3%)
  matrix products  10.8 us (2%)
  starting transfers between devices  4.84 us (1%)
    all_gather x4, waiting for transfers between devices, prefix_2(): gathered = jax.tree.map(lambda a: lax.all_gather(a, axis), part)  165 us
    add x63, other arithmetic, combine(): late_sim + late_are * early_sim + late_aim * early_sre  54.7 us
    mul x2, other arithmetic, pole_power(): magnitude * jnp.cos(rotation * powers)  24.9 us
    reduce_sum x1, other arithmetic, local(): jnp.sum(norm_factor * (residue_re * state_re - residue_im * state_im), ax...  21.4 us
    slice x1, local copies, waits for them, and re-layouts, local(): sum_re = summed[:, :, :modes]  11 us
    reshape x1, local copies, waits for them, and re-layouts, local(): lifted = lifted.reshape(nblocks, block_len, 2 * modes * channels)  11 us
    reshape x1, local copies, waits for them, and re-layouts, local(): summed = summed.reshape(nblocks, block_len, 2 * modes, channels)  10.8 us
    dot_general x1, matrix products, local(): jnp.einsum('bts,bsk->btk', within, lifted, precision=lax.Precision.HIGHEST)  10.8 us
  transfers between devices with their start and end apart: 8, of which 4 were waited for; matrix products, arithmetic and copies ran while one was open for 24% of the time, Pallas kernels for 0%

profile of v1, /device:TPU:249, one launch (start us, length us, event | category | flops | bytes accessed | tf_op | source)
XLA Modules:
  0.0 430.3 jit_solution(6462851792350326033)
XLA Ops:
  6.5 1.3 fusion.14
  10.5 9.6 %all_gather.43 = f32[2,4096]{1,0:T(2,128)S(1)} all-gather(f32[2,1024]{1,0:T(2,128)} %param.15), channel_id=1, replica_groups=mesh['dp'=4,'seq'=64] {'dp'}, dimensions={1}, use_global_device_ids=true | all-gather | bytes 40960 | tf_op jit(solution)/shard_map/all_gather | solution.py:62
  20.1 9.2 %all_gather.41 = f32[2,4096]{1,0:T(2,128)S(1)} all-gather(f32[2,1024]{1,0:T(2,128)} %param.14), channel_id=1, replica_groups=mesh['dp'=4,'seq'=64] {'dp'}, dimensions={1}, use_global_device_ids=true | all-gather | bytes 40960 | tf_op jit(solution)/shard_map/all_gather | solution.py:61
  29.3 1.7 multiply_bitcast_fusion
  31.0 1.0 slice.69
  32.0 1.3 collective-permute-start
  33.9 16.3 %cosine_multiply_fusion = (f32[32,2,4096]{2,1,0:T(2,128)}, f32[32,2,4096]{2,1,0:T(2,128)}) fusion(f32[2,4096]{1,0:T(2,128)S(1)} %get-tuple-element.233, f32[2,4096]{1,0:T(2,128)S(1)} %all_gather.41), kind=kLoop, calls=%fused_computation.37 | loop fusion | flops 1048576 | bytes 2162688 | tf_op jit(solution)/shard_map/mul | solution.py:49
  50.2 9.8 %all_gather.39 = f32[3,3,4096]{2,1,0:T(4,128)S(1)} all-gather(f32[3,3,1024]{2,1,0:T(4,128)} %param.13), channel_id=1, replica_groups=mesh['dp'=4,'seq'=64] {'dp'}, dimensions={2}, use_global_device_ids=true | all-gather | bytes 184320 | tf_op jit(solution)/shard_map/all_gather | solution.py:60
  60.0 8.5 %fusion.6 = (f32[32,2,4096]{2,0,1:T(8,128)S(1)}, f32[32,2,4096]{2,0,1:T(8,128)S(1)}, f32[32,2,4096]{2,0,1:T(8,128)}, f32[32,2,4096]{2,0,1:T(8,128)}) fusion(f32[32]{0:T(128)S(1)} %iota_add_fusion, f32[2,4096]{1,0:T(2,128)S(1)} %all_gather.43, f32[2,4096]{1,0:T(2,128)S(1)} %get-tuple-element.234), kind=kLoop, calls=%fused_computation.32 | loop fusion | flops 2097152 | bytes 4259968 | tf_op jit(solution)/shard_map/mul | solution.py:49
  68.7 2.7 maximum_bitcast_fusion
  71.4 2.1 multiply_add_fusion
  73.8 1.7 copy-done.4
  75.5 1.1 copy-done.5
  76.6 3.9 broadcast_multiply_fusion.1
  80.5 9.7 %pad_maximum_fusion = f32[4,32,4,4096]{3,2,1,0:T(4,128)} fusion(f32[4,32,2,4096]{3,2,1,0:T(2,128)} %get-tuple-element.218, f32[4,32,2,4096]{3,2,1,0:T(2,128)S(1)} %get-tuple-element.217), kind=kLoop, calls=%fused_computation.14 | loop fusion | flops 2097152 | bytes 16777216 | tf_op jit(solution)/shard_map/concatenate | solution.py:91
  90.2 11.0 %reshape.177 = f32[4,32,16384]{2,1,0:T(8,128)} reshape(f32[4,32,4,4096]{3,2,1,0:T(4,128)} %pad_maximum_fusion) | data formatting | bytes 16777216 | tf_op jit(solution)/shard_map/reshape | solution.py:92
  101.2 10.8 %fusion.8 = f32[4,32,16384]{2,1,0:T(8,128)} fusion(f32[4,32,16384]{2,1,0:T(8,128)} %reshape.177, s32[4,32]{1,0:T(4,128)S(1)} %sub.41, pred[32,32]{1,0:T(8,128)(4,1)S(1)} %iota_compare_fusion), kind=kOutput, calls=%fused_computation.48 | convolution fusion | flops 805314560 | bytes 16778752 | tf_op jit(solution)/shard_map/bts,bsk->btk/dot_general | solution.py:96
  112.1 10.8 %reshape.178 = f32[4,32,4,4096]{3,2,1,0:T(4,128)} reshape(f32[4,32,16384]{2,1,0:T(8,128)} %fusion.8) | data formatting | bytes 16777216 | tf_op jit(solution)/shard_map/reshape | solution.py:97
  122.9 11.0 %fusion.15 = (f32[4,32,2,4096]{3,2,1,0:T(2,128)S(1)}, f32[4,32,2,4096]{3,2,1,0:T(2,128)}) fusion(f32[4,32,4,4096]{3,2,1,0:T(4,128)} %reshape.178), kind=kLoop, calls=%fused_computation.79 | loop fusion | bytes 16777216 | tf_op jit(solution)/shard_map/slice | solution.py:98
  133.9 7.8 %multiply_subtract_fusion = (f32[4,32,2,4096]{3,1,2,0:T(8,128)S(1)}, f32[4,32,2,4096]{3,1,2,0:T(8,128)S(1)}) fusion(f32[4,32,2,4096]{3,2,1,0:T(2,128)} %get-tuple-element.216, f32[4,32,2,4096]{3,2,1,0:T(2,128)S(1)} %get-tuple-element.215, f32[32,2,4096]{2,0,1:T(8,128)S(1)} %copy-done.3, f32[32,2,4096]{2,0,1:T(8,128)} %get-tuple-element.225), kind=kLoop, calls=%fused_computation.22 | loop fusion | flops 6291456 | bytes 18874368 | tf_op jit(solution)/shard_map/sub | solution.py:100
  141.8 2.0 copy-done.1
  143.9 1.1 copy-done.2
  145.4 7.9 %while.33 = (s32[]{:T(128)}, f32[2,4096]{1,0:T(2,128)S(1)}, f32[2,4096]{1,0:T(2,128)S(1)}, f32[4,2,4096]{2,1,0:T(2,128)S(1)}, f32[4,2,4096]{2,1,0:T(2,128)}, /*i...) while((s32[]{:T(128)}, f32[2,4096]{1,0:T(2,128)S(1)}, ...), condition=%wide.region_3.4_spmd.clone, body=%wide.region_2.3_spmd.clone.sunk | while | flops 114691 | bytes 393876 | solution.py:114
  155.4 1.9 collective-permute-start.2
  157.3 9.0 %all_gather.42 = f32[2,4096]{1,0:T(2,128)S(1)} all-gather(f32[2,1024]{1,0:T(2,128)S(1)} %copy-done.8), channel_id=1, replica_groups=mesh['dp'=4,'seq'=64] {'dp'}, dimensions={1}, use_global_device_ids=true | all-gather | bytes 40960 | tf_op jit(solution)/shard_map/all_gather | solution.py:63
  166.4 9.0 %all_gather.40 = f32[4096]{0:T(1024)S(1)} all-gather(f32[1024]{0:T(1024)S(1)} %copy-done.10), channel_id=1, replica_groups=mesh['dp'=4,'seq'=64] {'dp'}, dimensions={0}, use_global_device_ids=true | all-gather | bytes 20480 | tf_op jit(solution)/shard_map/all_gather | solution.py:65
  176.1 3.4 collective-permute-done.3
  179.6 9.6 %all-gather.17.cloned.1.call-done = f32[64,2,4096]{2,1,0:T(2,128)} async-done(((f32[1,2,4096]{2,1,0:T(2,128)}), f32[64,2,4096]{2,1,0:T(2,128)}) %all-gather.17.cloned.1.call-update) | async-done | bytes 2097168 | tf_op jit(solution)/shard_map/all_gather | solution.py:36
  189.1 77.8 %all-gather.13.cloned.1.call-done = f32[64,2,4096]{2,1,0:T(2,128)} async-done(((f32[1,2,4096]{2,1,0:T(2,128)}), f32[64,2,4096]{2,1,0:T(2,128)}) %all-gather.13.cloned.1.call-update) | async-done | bytes 2097168 | tf_op jit(solution)/shard_map/all_gather | solution.py:36
  266.9 77.6 %all-gather.19.cloned.1.call-done = f32[64,2,4096]{2,1,0:T(2,128)} async-done(((f32[1,2,4096]{2,1,0:T(2,128)}), f32[64,2,4096]{2,1,0:T(2,128)}) %all-gather.19.cloned.1.call-update) | async-done | bytes 2097168 | tf_op jit(solution)/shard_map/all_gather | solution.py:36
  344.5 56.2 %while.32 = (s32[]{:T(128)}, f32[2,4096]{1,0:T(2,128)S(1)}, f32[2,4096]{1,0:T(2,128)S(1)}, s32[]{:T(128)}, f32[64,2,4096]{2,1,0:T(2,128)}, /*index=5*/f32[64,2,4...) while((s32[]{:T(128)}, f32[2,4096]{1,0:T(2,128)S(1)}, ...), condition=%wide.region_5.6_spmd, body=%wide.region_4.5_spmd.sunk | while | flops 65541 | bytes 262291 | solution.py:44
  344.5 0.9 fusion.18
  348.1 0.9 fusion.18
  350.8 0.9 fusion.18
  351.7 0.9 fusion.18
  354.4 0.9 fusion.18
  355.3 0.9 fusion.18
  357.9 0.9 fusion.18
  361.5 0.9 fusion.18
  365.1 0.9 fusion.18
  367.7 0.9 fusion.18
  368.6 0.9 fusion.18
  371.3 0.9 fusion.18
  372.2 0.9 fusion.18
  374.9 0.9 fusion.18
  378.4 0.9 fusion.18
  400.8 21.4 %multiply_reduce_fusion = f32[4,32,4096]{2,1,0:T(8,128)S(1)} fusion(f32[4,32,2,4096]{3,1,2,0:T(8,128)} %copy-done.2, f32[4,32,2,4096]{3,1,2,0:T(8,128)} %copy-done.1, f32[2,4096]{1,0:T(2,128)S(1)} %constant_dynamic-update-slice_fusion, f32[2,4096]{1,0:T(2,128)S(1)} %get-tuple-element.135, f32[2,4096]{1,0:T(2,128)S(1)} %get-tuple-element.134, ...), kind=kLoop, calls=%fused_computation.20 | loop fusion | flops 29884416 | bytes 13075968 | tf_op jit(solution)/shard_map/reduce_sum | solution.py:151
  422.2 1.6 fusion.5
  (125 shorter events, 55.2 us)
Async XLA Ops:
  6.5 173.0 %all-gather.15.cloned.1.call-start = ((), (), s32[]{:S(2)}) async-start(), calls=%async_computation.1 | async-start | bytes 2129920 | tf_op jit(solution)/shard_map/all_gather | solution.py:36
  31.0 158.1 %all-gather.17.cloned.1.call-start = ((), (), s32[]{:S(2)}) async-start(), calls=%async_computation.2 | async-start | bytes 2129920 | tf_op jit(solution)/shard_map/all_gather | solution.py:36
  32.0 36.7 %collective-permute-start = (bf16[3,1,2,4096]{3,2,0,1:T(2,128)(2,1)S(1)}, bf16[3,1,2,4096]{3,2,0,1:T(2,128)(2,1)S(1)}, u32[]{:S(2)}, u32[]{:S(2)}) collective-permute-start(bf16[3,1,2,4096]{3,2,0,1:T(2,128)(2,1)S(1)} %slice.69), channel_id=1, source_target_pairs={{0,1},{1,2},{2,3},{3,4},{4,5},{5,6},{6,7},{7,8},{8,9},{9,10},{10,1... | collective-permute-start | bytes 147464 | tf_op jit(solution)/shard_map/ppermute | solution.py:31
  33.3 233.5 %all-gather.13.cloned.1.call-start = ((), (), s32[]{:S(2)}) async-start(), calls=%async_computation | async-start | bytes 2129920 | tf_op jit(solution)/shard_map/all_gather | solution.py:36
  73.5 7.0 %copy-start = (f32[3,128,4096]{2,1,0:T(8,128)}, f32[3,128,4096]{2,1,0:T(8,128)S(1)}, u32[]{:S(2)}) copy-start(f32[3,128,4096]{2,1,0:T(8,128)S(1)} %multiply_add_fusion) | copy-start | bytes 18874372
  73.5 2.0 copy-start.4
  73.5 3.1 copy-start.5
  122.9 11.0 %copy-start.3 = (f32[32,2,4096]{2,0,1:T(8,128)S(1)}, f32[32,2,4096]{2,0,1:T(8,128)}, u32[]{:S(2)}) copy-start(f32[32,2,4096]{2,0,1:T(8,128)} %get-tuple-element.224) | copy-start | bytes 3145732
  133.9 20.6 %copy-start.9 = (f32[2,1024]{1,0:T(2,128)S(1)}, f32[2,1024]{1,0:T(2,128)}, u32[]{:S(2)}) copy-start(f32[2,1024]{1,0:T(2,128)} %param.17) | copy-start | bytes 24580
  133.9 23.3 %copy-start.8 = (f32[2,1024]{1,0:T(2,128)S(1)}, f32[2,1024]{1,0:T(2,128)}, u32[]{:S(2)}) copy-start(f32[2,1024]{1,0:T(2,128)} %param.16) | copy-start | bytes 24580
  133.9 32.5 %copy-start.10 = (f32[1024]{0:T(1024)S(1)}, f32[1024]{0:T(1024)}, u32[]{:S(2)}) copy-start(f32[1024]{0:T(1024)} %param.18) | copy-start | bytes 12292
  141.8 2.0 copy-start.1
  141.8 3.3 copy-start.2
  153.3 0.6 copy-start.6
  153.3 0.7 copy-start.7
  153.9 190.6 %all-gather.19.cloned.1.call-start = ((), (), s32[]{:S(2)}) async-start(), calls=%async_computation.3 | async-start | bytes 2129920 | tf_op jit(solution)/shard_map/all_gather | solution.py:36
  154.5 20.9 %collective-permute-start.1 = (f32[2,1024]{1,0:T(2,128)S(1)}, f32[2,1024]{1,0:T(2,128)S(1)}, u32[]{:S(2)}, u32[]{:S(2)}) collective-permute-start(f32[2,1024]{1,0:T(2,128)S(1)} %copy-done.9), channel_id=1, source_target_pairs={{0,64},{64,128},{128,192},{192,0},{1,65},{65,129},{129,193},{193,1... | collective-permute-start | bytes 24584 | tf_op jit(solution)/shard_map/ppermute | solution.py:18
  155.4 20.8 %collective-permute-start.2 = (f32[2,1024]{1,0:T(2,128)S(1)}, f32[2,1024]{1,0:T(2,128)S(1)}, u32[]{:S(2)}, u32[]{:S(2)}) collective-permute-start(f32[2,1024]{1,0:T(2,128)S(1)} %copy-done.9), channel_id=1, source_target_pairs={{0,192},{64,0},{128,64},{192,128},{1,193},{65,1},{129,65},{193,129... | collective-permute-start | bytes 24584 | tf_op jit(solution)/shard_map/ppermute | solution.py:21
  175.4 4.1 collective-permute-start.3
  400.7 21.4 %slice-start = ((s8[6291456]{0:T(1024)(128)(4,1)}), s8[4194304]{0:T(1024)(128)(4,1)S(1)}, s32[]{:S(2)}) async-start(s8[6291456]{0:T(1024)(128)(4,1)} %bitcast.73), calls=%async_computation.4 | async-start | bytes 8388608
  400.7 21.4 %slice-start.1 = ((s8[6291456]{0:T(1024)(128)(4,1)}), s8[2097152]{0:T(1024)(128)(4,1)S(1)}, s32[]{:S(2)}) async-start(s8[6291456]{0:T(1024)(128)(4,1)} %bitcast.73), calls=%async_computation.5 | async-start | bytes 4194304
Sparse Core Ops, SparseCore 0:
  31.1 80.1 all-gather.14
  114.1 74.9 all-gather.16
  191.9 74.9 all-gather.12
  269.5 74.9 all-gather.18
